TPU v7x, 512 devices: a whole 4x8x8 slice. The times are simulated.
512 devices in a mesh: cam: 16 (over x_lo, y), space: 32 (over x_hi, z, core).
Axes of the slice: x: 4 (x_hi: 2, x_lo: 2; x = x_hi * 2 + x_lo), y: 8, z: 8, core: 2. Of those that a mesh axis runs over, the one named last changes fastest.
Arguments:
- features: float32 [64, 131072], P(None, ('cam', 'space')), may hold values from -6 to 6
- positions: float32 [3, 131072], P(None, ('cam', 'space')), may hold values from -6144 to 6144, as said below
- spreads: float32 [131072], P(('cam', 'space')), may hold values from 16 to 64
- logits: float32 [131072], P(('cam', 'space')), may hold values from -6 to -2
- camera: float32 [16, 3], replicated, may hold values from -1 to 1
- decoder: bfloat16 [64, 512], replicated, may hold values from -0.75 to 0.75
- tile_lists: int32 [16, 32, 16, 256], P('cam', 'space'), may hold values from 0 to 8191, as said below
- counts: int32 [16, 32, 16], P('cam', 'space'), may hold values from 1 to 256, as said below
- targets: bfloat16 [16, 32, 16, 256, 512], P('cam', 'space'), may hold values from -6 to 6
Outputs:
- grad_features: float32 [64, 131072], P(None, ('cam', 'space'))
- grad_logits: float32 [131072], P(('cam', 'space'))
Inputs may be any that keep to these rules, and one draw needn't show every extreme that they name: `positions`: rows are x, y and depth; depth lies between 4 and 8. `tile_lists`: the list of tile (c, s, j) names only ids j * 256 + q or 4096 + j * 256 + q with 0 <= q < 256, no id twice; lists of tile row 0 name only ids below 4096. `counts`: some tile has all 256 entries live.
All inputs are finite; a program needn't handle non-finite values.
Results may differ from a plain program's by a relative error of at most 0.003.
Values may be sent and summed in bfloat16 or wider, within the bound.
No kernel may reach another device: no remote copies, remote signals or barrier semaphores. Data moves between devices by JAX's collectives and lax.ppermute only.
A program may use at most 64 MiB of HBM per device.

v0:
```python
import jax
import jax.numpy as jnp
from jax import lax
from jax.sharding import PartitionSpec as P

TS = 16


def shifted(shard, axis, by):
    length = lax.axis_size(axis)
    pairs = [(i, i + by) for i in range(length) if 0 <= i + by < length]
    return lax.ppermute(shard, axis, pairs)


def project_terms(
    gathered, viewers, tile_row, columns, live_counts, grad_maker, image_width, image_height
):
    channels = gathered.shape[0] - 5
    tiles_here = gathered.shape[1]
    length = gathered.shape[2]
    step_len = 128
    block_count = length // step_len
    pixel_count = TS * TS
    feature_bf = gathered[:channels].astype(jnp.bfloat16)
    distance = gathered[channels + 2] - 0.05 * viewers[:, 2:3]
    centre_u = (gathered[channels] - 0.75 * TS * viewers[:, 0:1]) / distance + 0.5 * image_width
    centre_v = (
        gathered[channels + 1] - 0.75 * TS * viewers[:, 1:2]
    ) / distance + 0.5 * image_height
    radius = gathered[channels + 3] / distance
    sigmoid_open = jax.nn.sigmoid(gathered[channels + 4])
    opacity = 0.99 * sigmoid_open
    sigmoid_slope = 0.99 * sigmoid_open * (1.0 - sigmoid_open)
    pixel_id = jnp.arange(pixel_count, dtype=jnp.int32)
    pixel_u = (columns[:, None] * TS + pixel_id[None, :] % TS).astype(jnp.float32) + 0.5
    pixel_v = (tile_row * TS + pixel_id // TS).astype(jnp.float32) + 0.5
    alive_mask = (jnp.arange(length, dtype=jnp.int32)[None, :] < live_counts[:, None]).astype(
        jnp.float32
    )
    logit_gate_all = alive_mask * sigmoid_slope
    steps_used = (jnp.max(live_counts) + step_len - 1) // step_len

    def block_terms(first_entry):

        def window_of(source_array):
            return lax.dynamic_slice_in_dim(
                source_array, first_entry, step_len, axis=source_array.ndim - 1
            )

        delta_u = pixel_u[:, :, None] - window_of(centre_u)[:, None, :]
        delta_v = pixel_v[None, :, None] - window_of(centre_v)[:, None, :]
        spread = window_of(radius)[:, None, :]
        falloff = jnp.exp(-(delta_u * delta_u + delta_v * delta_v) / (2.0 * spread * spread))
        opaque = (window_of(opacity) * window_of(alive_mask))[:, None, :] * falloff
        log_keep = jnp.log(1.0 - opaque)
        inner_log = jnp.cumsum(log_keep, axis=2) - log_keep
        return (
            falloff,
            opaque,
            log_keep,
            inner_log,
            window_of(feature_bf),
            window_of(logit_gate_all),
        )

    def forward(position, state_in):
        log_start, feature_sum, starts = state_in
        first_entry = position * step_len
        falloff, opaque, log_keep, inner_log, block_feat, unused = block_terms(first_entry)
        weight = opaque * jnp.exp(log_start[:, :, None] + inner_log)
        feature_sum = feature_sum + jnp.einsum(
            "tpk,ctk->tcp",
            weight.astype(jnp.bfloat16),
            block_feat,
            preferred_element_type=jnp.float32,
        )
        starts = lax.dynamic_update_index_in_dim(starts, log_start, position, 0)
        return (log_start + jnp.sum(log_keep, axis=2), feature_sum, starts)

    initial = (
        jnp.zeros((tiles_here, pixel_count), jnp.float32),
        jnp.zeros((tiles_here, channels, pixel_count), jnp.float32),
        jnp.zeros((block_count, tiles_here, pixel_count), jnp.float32),
    )
    unused_log, feature_sum, starts = lax.fori_loop(0, steps_used, forward, initial)
    composite = feature_sum.astype(jnp.bfloat16)
    pixel_grad = grad_maker(composite).astype(jnp.bfloat16)

    def backward(reverse_turn, state_in):
        behind_sum, feature_grad, logit_grad = state_in
        position = steps_used - 1 - reverse_turn
        first_entry = position * step_len
        falloff, opaque, log_keep, inner_log, block_feat, logit_gate = block_terms(first_entry)
        keep_to = jnp.exp(
            lax.dynamic_index_in_dim(starts, position, 0, keepdims=False)[:, :, None] + inner_log
        )
        weight = opaque * keep_to
        weight_bf = weight.astype(jnp.bfloat16)
        contrib = jnp.einsum(
            "tcp,ctk->tpk", pixel_grad, block_feat, preferred_element_type=jnp.float32
        )
        weighted = weight * contrib
        block_total = jnp.sum(weighted, axis=2)
        behind = behind_sum[:, :, None] + block_total[:, :, None] - jnp.cumsum(weighted, axis=2)
        dopaque = keep_to * contrib - behind / (1.0 - opaque)
        logit_part = logit_gate * jnp.sum(dopaque * falloff, axis=1)
        feature_part = jnp.einsum(
            "tpk,tcp->ctk", weight_bf, pixel_grad, preferred_element_type=jnp.float32
        )
        feature_grad = lax.dynamic_update_slice_in_dim(
            feature_grad, feature_part, first_entry, axis=2
        )
        logit_grad = lax.dynamic_update_slice_in_dim(logit_grad, logit_part, first_entry, axis=1)
        return (behind_sum + block_total, feature_grad, logit_grad)

    initial_back = (
        jnp.zeros((tiles_here, pixel_count), jnp.float32),
        jnp.zeros((channels, tiles_here, length), jnp.float32),
        jnp.zeros((tiles_here, length), jnp.float32),
    )
    unused_behind, feature_grad, logit_grad = lax.fori_loop(0, steps_used, backward, initial_back)
    return (feature_grad, logit_grad)


def full_target_rule(pixel_targets, decoder):
    decoder_wide = decoder.astype(jnp.float32)

    def make_grad(composite):
        decoded = jnp.einsum("tcp,cd->tpd", composite, decoder, preferred_element_type=jnp.float32)
        residual = decoded - pixel_targets.astype(jnp.float32)
        return jnp.einsum("tpd,cd->tcp", residual, decoder_wide, precision=lax.Precision.HIGHEST)

    return make_grad


def on_device(features, positions, spreads, logits, camera, decoder, tile_lists, counts, targets):
    channels = features.shape[0]
    length = features.shape[1]
    camera_count = lax.axis_size("cam")
    space_count = lax.axis_size("space")
    camera_id = lax.axis_index("cam")
    tile_row = lax.axis_index("space")
    image_width = TS * camera_count
    image_height = TS * space_count
    block_rows = camera_count * length
    own_slab = jnp.concatenate([features, positions, spreads[None], logits[None]], axis=0)
    upper_slab = shifted(own_slab, "space", 1)
    both_slabs = lax.all_gather(jnp.stack([own_slab, upper_slab]), "cam", axis=2, tiled=True)
    gauss_table = jnp.concatenate([both_slabs[0], both_slabs[1]], axis=1)
    entries = tile_lists[0, 0]
    picker = (jnp.arange(camera_count, dtype=jnp.int32) == camera_id).astype(jnp.float32)
    viewers = jnp.broadcast_to(jnp.sum(camera * picker[:, None], axis=0), (camera_count, 3))
    columns = jnp.arange(camera_count, dtype=jnp.int32)
    gathered = jnp.take(gauss_table, entries, axis=1)
    grad_maker = full_target_rule(targets[0, 0], decoder)
    feature_grad, logit_grad = project_terms(
        gathered, viewers, tile_row, columns, counts[0, 0], grad_maker, image_width, image_height
    )
    values = jnp.concatenate([feature_grad, logit_grad[None]], axis=0)
    totals = jnp.zeros((channels + 1, 2 * block_rows), jnp.float32).at[:, entries].add(values)
    returned = shifted(totals[:, block_rows:], "space", -1)
    summed = lax.psum_scatter(
        totals[:, :block_rows] + returned, "cam", scatter_dimension=1, tiled=True
    )
    return (summed[:channels], summed[channels])


def solution(mesh):
    placed = (
        P(None, ("cam", "space")),
        P(None, ("cam", "space")),
        P(("cam", "space")),
        P(("cam", "space")),
        P(),
        P(),
        P("cam", "space", None, None),
        P("cam", "space", None),
        P("cam", "space", None, None, None),
    )
    return jax.shard_map(
        on_device,
        mesh=mesh,
        in_specs=placed,
        out_specs=(P(None, ("cam", "space")), P(("cam", "space"))),
        check_vma=False,
    )
```

profile of v0, /device:TPU:4, one launch (start us, length us, event | category | flops | bytes accessed | tf_op | source)
XLA Modules:
  0.0 300.1 jit_solution(15788181093214662596)
XLA Ops:
  7.3 0.9 copy.57
  8.2 0.8 copy.58
  9.0 0.8 copy.59
  9.8 0.8 copy.60
  10.8 1.9 collective-permute-start
  12.9 10.9 %collective-permute-done = f32[69,256]{0,1:T(8,128)S(1)} collective-permute-done((f32[69,256]{0,1:T(8,128)S(1)}, f32[69,256]{0,1:T(8,128)S(1)}, u32[]{:S(2)}, u32[]{:S(2)}) %collective-permute-start) | collective-permute-done | bytes 70688 | tf_op jit(solution)/shard_map/ppermute | solution.py:12
  23.8 0.7 pad_maximum_fusion.1
  24.6 0.6 reduce_max.9
  26.1 0.7 fusion.62
  28.9 72.8 %all-gather.2.cloned.1.call-done = f32[2,69,4096]{1,2,0:T(8,128)} async-done(((f32[2,69,256]{1,2,0:T(8,128)}), f32[2,69,4096]{1,2,0:T(8,128)}) %all-gather.2.cloned.1.call-update) | async-done | bytes 2261008 | tf_op jit(solution)/shard_map/all_gather | solution.py:148
  101.7 2.5 slice_bitcast_fusion.1
  104.2 2.2 pad_maximum_fusion
  106.4 13.0 %gather_fusion = f32[4096,69]{1,0:T(8,128)S(1)} fusion(f32[69,8192]{0,1:T(8,128)} %pad_maximum_fusion, s32[4096]{0:T(1024)S(1)} %broadcast_clamp_fusion), kind=kCustom, calls=%fused_computation | custom fusion | bytes 2277376 | tf_op jit(solution)/shard_map/jit(_take)/gather | solution.py:154
  119.3 1.0 copy.61
  121.0 11.3 %while.32 = (s32[]{:T(128)}, f32[16,256]{1,0:T(8,128)S(1)}, f32[16,64,256]{2,1,0:T(8,128)S(1)}, f32[2,16,256]{2,1,0:T(8,128)S(1)}, s32[]{:T(128)}, /*index=5*/f3...) while((s32[]{:T(128)}, f32[16,256]{1,0:T(8,128)S(1)}, ...), condition=%wide.region_5.6_spmd.clone, body=%wide.region_2.5_spmd.clone.sunk | while | flops 150754048 | bytes 4895069 | solution.py:85
  121.7 1.5 fusion.84
  123.1 2.8 multiply_convert_fusion.2
  126.0 0.5 convolution_add_fusion.2
  127.2 1.5 fusion.84
  128.7 2.8 multiply_convert_fusion.2
  131.5 0.5 convolution_add_fusion.2
  132.3 1.3 fusion.44
  133.5 0.9 copy-done.1
  134.4 4.9 %fusion.43 = bf16[16,64,256]{2,1,0:T(8,128)(2,1)S(1)} fusion(f32[16,256,512]{2,1,0:T(8,128)S(1)} %fusion.44, bf16[1,1,16,256,512]{4,3,2,1,0:T(8,128)(2,1)S(1)} %copy-done.1, bf16[64,512]{1,0:T(8,128)(2,1)S(1)} %copy-done), kind=kOutput, calls=%fused_computation.78 | convolution fusion | flops 1615069184 | bytes 13172736 | tf_op jit(solution)/shard_map/tpd,cd->tcp/dot_general | solution.py:131
  139.4 25.9 %while.33 = (s32[]{:T(128)}, f32[16,256]{1,0:T(8,128)S(1)}, f32[64,16,256]{2,0,1:T(8,128)S(1)}, f32[16,256]{1,0:T(8,128)S(1)}, s32[]{:T(128)}, /*index=5*/s32[]{...) while((s32[]{:T(128)}, f32[16,256]{1,0:T(8,128)S(1)}, ...), condition=%wide.region_11.12_spmd.clone, body=%wide.region_6.11_spmd.clone.sunk | while | flops 295195392 | bytes 27490700 | solution.py:121
  139.8 1.2 subtract_log_fusion.8
  141.0 1.3 fusion.91
  142.3 2.2 fusion.93
  144.5 2.5 fusion.92
  147.0 1.3 fusion.94
  148.2 4.2 %fusion.95 = f32[16,128]{1,0:T(8,128)S(1)} fusion(f32[16,128,256]{2,1,0:T(8,128)S(1)} %get-tuple-element.746, f32[16,256,128]{1,0,2:T(8,128)S(1)} %fusion.94, f32[16,256]{1,0:T(8,128)S(1)} %add.491, f32[16,128]{1,0:T(8,128)S(1)} %get-tuple-element.741, f32[16,128]{1,0:T(8,128)S(1)} %get-tuple-element.742, f32[256]{0:T(256)S(1)} %fusion.90, ...), kind=kLoop, calls=%fused_computation.35.clone.1 | loop fusion | flops 8910848 | bytes 6382592 | tf_op jit(solution)/shard_map/while/body/reduce_sum | solution.py:106
  152.6 1.2 subtract_log_fusion.8
  153.8 1.3 fusion.91
  155.1 2.2 fusion.93
  157.3 2.5 fusion.92
  159.8 1.3 fusion.94
  161.1 4.2 %fusion.95 = f32[16,128]{1,0:T(8,128)S(1)} fusion(f32[16,128,256]{2,1,0:T(8,128)S(1)} %get-tuple-element.746, f32[16,256,128]{1,0,2:T(8,128)S(1)} %fusion.94, f32[16,256]{1,0:T(8,128)S(1)} %add.491, f32[16,128]{1,0:T(8,128)S(1)} %get-tuple-element.741, f32[16,128]{1,0:T(8,128)S(1)} %get-tuple-element.742, f32[256]{0:T(256)S(1)} %fusion.90, ...), kind=kLoop, calls=%fused_computation.35.clone.1 | loop fusion | flops 8910848 | bytes 6382592 | tf_op jit(solution)/shard_map/while/body/reduce_sum | solution.py:106
  165.5 0.8 copy.76
  166.3 24.5 %scatter_custom_fusion = f32[65,8192]{0,1:T(8,128)} fusion(s32[4096]{0:T(1024)S(1)} %bitcast.99, f32[4096,65]{1,0:T(8,128)S(1)} %bitcast.95, f32[]{:T(128)} %constant.142.clone.1), kind=kCustom, calls=%fused_computation.75 | custom fusion | flops 266240 | bytes 2129924 | tf_op jit(solution)/shard_map/scatter-add | solution.py:160
  190.8 1.6 slice-done
  192.4 0.9 copy.72
  193.3 1.9 collective-permute-start.1
  195.2 13.7 %collective-permute-done.1 = f32[65,4096]{1,0:T(8,128)} collective-permute-done((f32[65,4096]{1,0:T(8,128)S(1)}, f32[65,4096]{1,0:T(8,128)}, u32[]{:S(2)}, u32[]{:S(2)}) %collective-permute-start.1) | collective-permute-done | bytes 1064992 | tf_op jit(solution)/shard_map/ppermute | solution.py:12
  208.9 1.8 copy.73
  210.7 3.1 %slice_add_fusion = f32[65,4096]{0,1:T(8,128)} fusion(f32[65,4096]{0,1:T(8,128)S(1)} %copy.73, f32[65,8192]{0,1:T(8,128)} %scatter_custom_fusion), kind=kLoop, calls=%fused_computation.72 | loop fusion | flops 266240 | bytes 3194880 | tf_op jit(solution)/shard_map/add | solution.py:163
  213.9 76.1 %reduce-scatter.2.cloned.1.call-done = f32[65,256]{0,1:T(8,128)} async-done(((f32[65,4096]{0,1:T(8,128)}), f32[65,256]{0,1:T(8,128)}) %reduce-scatter.2.cloned.1.call-update) | async-done | bytes 66576 | tf_op jit(solution)/shard_map/reduce_scatter | solution.py:162
  290.0 1.6 copy.74
  291.6 1.7 slice_reduce_fusion
  (80 shorter events, 3.0 us)
Async XLA Ops:
  7.2 125.1 %copy-start = (bf16[64,512]{1,0:T(8,128)(2,1)S(1)}, bf16[64,512]{1,0:T(8,128)(2,1)}, u32[]{:S(2)}) copy-start(bf16[64,512]{1,0:T(8,128)(2,1)} %param.18) | copy-start | bytes 196612
  7.2 17.4 %copy-start.3 = (s32[1,1,16]{2,1,0:T(1,128)S(1)}, s32[1,1,16]{2,1,0:T(1,128)}, u32[]{:S(2)}) copy-start(s32[1,1,16]{2,1,0:T(1,128)} %param.20) | copy-start | bytes 196
  7.2 18.7 %copy-start.4 = (f32[16,3]{0,1:T(4,128)S(1)}, f32[16,3]{0,1:T(4,128)}, u32[]{:S(2)}) copy-start(f32[16,3]{0,1:T(4,128)} %param.17) | copy-start | bytes 580
  7.2 20.9 %copy-start.2 = (s32[1,1,16,256]{3,2,1,0:T(8,128)S(1)}, s32[1,1,16,256]{3,2,1,0:T(8,128)}, u32[]{:S(2)}) copy-start(s32[1,1,16,256]{3,2,1,0:T(8,128)} %param.19) | copy-start | bytes 49156
  7.2 94.5 %all-gather.2.cloned.1.call-start = ((), (), s32[]{:S(2)}) async-start(), calls=%async_computation.1 | async-start | bytes 4456448 | tf_op jit(solution)/shard_map/all_gather | solution.py:148
  10.8 13.0 %collective-permute-start = (f32[69,256]{0,1:T(8,128)S(1)}, f32[69,256]{0,1:T(8,128)S(1)}, u32[]{:S(2)}, u32[]{:S(2)}) collective-permute-start(f32[69,256]{0,1:T(8,128)S(1)} %pad_maximum_fusion.2), channel_id=1, source_target_pairs={{0,1},{1,2},{2,3},{3,4},{4,5},{5,6},{6,7},{7,8},{8,9},{9,10},{10,1... | collective-permute-start | bytes 211976 | tf_op jit(solution)/shard_map/ppermute | solution.py:12
  24.5 265.5 %reduce-scatter.2.cloned.1.call-start = ((), (), s32[]{:S(2)}) async-start(), calls=%async_computation.2 | async-start | bytes 2228224 | tf_op jit(solution)/shard_map/reduce_scatter | solution.py:162
  132.2 2.2 copy-start.1
  190.8 1.6 slice-start
  193.3 15.6 %collective-permute-start.1 = (f32[65,4096]{1,0:T(8,128)S(1)}, f32[65,4096]{1,0:T(8,128)}, u32[]{:S(2)}, u32[]{:S(2)}) collective-permute-start(f32[65,4096]{1,0:T(8,128)S(1)} %copy.72), channel_id=1, source_target_pairs={{1,0},{2,1},{3,2},{4,3},{5,4},{6,5},{7,6},{8,7},{9,8},{10,9},{11,1... | collective-permute-start | bytes 3194888 | tf_op jit(solution)/shard_map/ppermute | solution.py:12
Sparse Core Ops, SparseCore 0:
  24.7 76.9 all-gather.1
  214.0 75.9 reduce-scatter.1
where the time goes:
time: 301 us; the launch traced here: 300 us
  waiting for transfers between devices  174 us (58%)
  other arithmetic  56.9 us (19%)
  local copies, waits for them, and re-layouts  31.3 us (10%)
  between operations  17.1 us (6%)
  matrix products  16.6 us (6%)
  starting transfers between devices  3.92 us (1%)
    reduce_scatter x1, waiting for transfers between devices, on_device(): lax.psum_scatter(totals[:, :block_rows] + returned, 'cam', scatter_dimens...  76.1 us
    all_gather x1, waiting for transfers between devices, on_device(): lax.all_gather(jnp.stack([own_slab, upper_slab]), 'cam', axis=2, tiled=True)  72.8 us
    ppermute x2, waiting for transfers between devices, shifted(): return lax.ppermute(shard, axis, pairs)  24.6 us
    scatter-add x1, other arithmetic, on_device(): jnp.zeros((channels + 1, 2 * block_rows), jnp.float32).at[:, entries]  24.5 us
    gather x2, local copies, waits for them, and re-layouts, on_device(): gathered = jnp.take(gauss_table, entries, axis=1)  14 us
    reduce_sum x2, other arithmetic, backward(): logit_part = logit_gate * jnp.sum(dopaque * falloff, axis=1)  8.48 us
    another operation x4, other arithmetic, block_terms(): inner_log = jnp.cumsum(log_keep, axis=2) - log_keep  8.17 us
  transfers between devices with their start and end apart: 4, of which 4 were waited for; matrix products, arithmetic and copies ran while one was open for 1% of the time, Pallas kernels for 0%

commit v1 on v0

--- a/solution.py
+++ b/solution.py
@@ -145,7 +145,7 @@
     block_rows = camera_count * length
     own_slab = jnp.concatenate([features, positions, spreads[None], logits[None]], axis=0)
     upper_slab = shifted(own_slab, "space", 1)
-    both_slabs = lax.all_gather(jnp.stack([own_slab, upper_slab]), "cam", axis=2, tiled=True)
+    both_slabs = jnp.concatenate(lax.all_gather(jnp.stack([own_slab, upper_slab]), "cam"), axis=2)
     gauss_table = jnp.concatenate([both_slabs[0], both_slabs[1]], axis=1)
     entries = tile_lists[0, 0]
     picker = (jnp.arange(camera_count, dtype=jnp.int32) == camera_id).astype(jnp.float32)

time: 301 us -> 298 us (0.990)
  waiting for transfers between devices: 174 us -> 165 us
  other arithmetic: 56.9 us -> 60.9 us
    all_gather x1, waiting for transfers between devices: 72.8 us -> 65.6 us  [on_device(): lax.all_gather(jnp.stack([own_slab, upper_slab]), 'cam')]
    all_gather x0 -> x1, local copies, waits for them, and re-layouts: none -> 4.7 us  [on_device(): lax.all_gather(jnp.stack([own_slab, upper_slab]), 'cam')]
  transfers between devices with their start and end apart: 4 -> 4, of which waited for: 4 -> 4; matrix products, arithmetic and copies ran while one was open for 1% -> 2% of each run, Pallas kernels for 0% -> 0%
where the time goes in v1:
time: 298 us; the launch traced here: 297 us
  waiting for transfers between devices  165 us (55%)
  other arithmetic  60.9 us (20%)
  local copies, waits for them, and re-layouts  32.8 us (11%)
  between operations  16.9 us (6%)
  matrix products  16.6 us (6%)
  starting transfers between devices  3.92 us (1%)
    reduce_scatter x1, waiting for transfers between devices, on_device(): lax.psum_scatter(totals[:, :block_rows] + returned, 'cam', scatter_dimens...  75.5 us
    all_gather x1, waiting for transfers between devices, on_device(): lax.all_gather(jnp.stack([own_slab, upper_slab]), 'cam')  65.6 us
    scatter-add x1, other arithmetic, on_device(): jnp.zeros((channels + 1, 2 * block_rows), jnp.float32).at[:, entries]  24.5 us
    ppermute x2, waiting for transfers between devices, shifted(): return lax.ppermute(shard, axis, pairs)  24.1 us
    gather x2, local copies, waits for them, and re-layouts, on_device(): gathered = jnp.take(gauss_table, entries, axis=1)  14 us
    reduce_sum x2, other arithmetic, backward(): logit_part = logit_gate * jnp.sum(dopaque * falloff, axis=1)  8.48 us
    another operation x4, other arithmetic, block_terms(): inner_log = jnp.cumsum(log_keep, axis=2) - log_keep  8.17 us
  transfers between devices with their start and end apart: 4, of which 4 were waited for; matrix products, arithmetic and copies ran while one was open for 2% of the time, Pallas kernels for 0%

profile of v1, /device:TPU:4, one launch (start us, length us, event | category | flops | bytes accessed | tf_op | source)
XLA Modules:
  0.0 297.1 jit_solution(16496471256614473071)
XLA Ops:
  7.2 0.9 fusion.61
  8.1 1.9 collective-permute-start
  10.1 10.4 %collective-permute-done = f32[69,256]{1,0:T(8,128)S(1)} collective-permute-done((f32[69,256]{1,0:T(8,128)S(1)}, f32[69,256]{1,0:T(8,128)S(1)}, u32[]{:S(2)}, u32[]{:S(2)}) %collective-permute-start) | collective-permute-done | bytes 70688 | tf_op jit(solution)/shard_map/ppermute | solution.py:12
  20.5 0.7 pad_maximum_fusion.1
  21.2 1.3 reduce_max.9
  23.2 0.8 multiply_reduce_fusion
  24.0 0.7 fusion.64
  25.9 0.7 fusion.48
  27.4 0.7 fusion.60
  28.1 0.7 compare_and_fusion
  28.8 65.6 %all-gather.3.cloned.1.call-done = f32[32,69,256]{2,1,0:T(8,128)} async-done(((f32[2,69,256]{2,1,0:T(8,128)}), f32[32,69,256]{2,1,0:T(8,128)}) %all-gather.3.cloned.1.call-update) | async-done | bytes 2261008 | tf_op jit(solution)/shard_map/all_gather | solution.py:148
  94.4 4.7 %copy.53 = f32[16,2,69,256]{2,3,0,1:T(8,128)} copy(f32[16,2,69,256]{3,2,1,0:T(8,128)} %bitcast.98) | data formatting | bytes 4521984 | tf_op jit(solution)/shard_map/all_gather | solution.py:148
  99.1 2.6 fusion.63
  101.8 2.2 pad_maximum_fusion
  104.0 13.0 %gather_fusion = f32[4096,69]{1,0:T(8,128)S(1)} fusion(f32[69,8192]{0,1:T(8,128)} %pad_maximum_fusion, s32[4096]{0:T(1024)S(1)} %broadcast_clamp_fusion), kind=kCustom, calls=%fused_computation | custom fusion | bytes 2277376 | tf_op jit(solution)/shard_map/jit(_take)/gather | solution.py:154
  117.0 1.0 copy.54
  118.6 11.3 %while.32 = (s32[]{:T(128)}, f32[16,256]{1,0:T(8,128)S(1)}, f32[16,64,256]{2,1,0:T(8,128)S(1)}, f32[2,16,256]{2,1,0:T(8,128)S(1)}, s32[]{:T(128)}, /*index=5*/f3...) while((s32[]{:T(128)}, f32[16,256]{1,0:T(8,128)S(1)}, ...), condition=%wide.region_5.6_spmd.clone, body=%wide.region_2.5_spmd.clone.sunk | while | flops 150754048 | bytes 4895069 | solution.py:85
  119.3 1.5 fusion.85
  120.7 2.8 multiply_convert_fusion.2
  124.8 1.5 fusion.85
  126.3 2.8 multiply_convert_fusion.2
  129.9 1.3 fusion.44
  131.2 0.9 copy-done.1
  132.1 4.9 %fusion.43 = bf16[16,64,256]{2,1,0:T(8,128)(2,1)S(1)} fusion(f32[16,256,512]{2,1,0:T(8,128)S(1)} %fusion.44, bf16[1,1,16,256,512]{4,3,2,1,0:T(8,128)(2,1)S(1)} %copy-done.1, bf16[64,512]{1,0:T(8,128)(2,1)S(1)} %copy-done), kind=kOutput, calls=%fused_computation.76 | convolution fusion | flops 1615069184 | bytes 13172736 | tf_op jit(solution)/shard_map/tpd,cd->tcp/dot_general | solution.py:131
  137.1 25.9 %while.33 = (s32[]{:T(128)}, f32[16,256]{1,0:T(8,128)S(1)}, f32[64,16,256]{2,0,1:T(8,128)S(1)}, f32[16,256]{1,0:T(8,128)S(1)}, s32[]{:T(128)}, /*index=5*/s32[]{...) while((s32[]{:T(128)}, f32[16,256]{1,0:T(8,128)S(1)}, ...), condition=%wide.region_11.12_spmd.clone, body=%wide.region_6.11_spmd.clone.sunk | while | flops 295195392 | bytes 27490700 | solution.py:121
  137.4 1.2 subtract_log_fusion.8
  138.6 1.3 fusion.92
  139.9 2.2 fusion.94
  142.1 2.5 fusion.93
  144.6 1.3 fusion.95
  145.8 4.2 %fusion.96 = f32[16,128]{1,0:T(8,128)S(1)} fusion(f32[16,128,256]{2,1,0:T(8,128)S(1)} %get-tuple-element.748, f32[16,256,128]{1,0,2:T(8,128)S(1)} %fusion.95, f32[16,256]{1,0:T(8,128)S(1)} %add.491, f32[16,128]{1,0:T(8,128)S(1)} %get-tuple-element.743, f32[16,128]{1,0:T(8,128)S(1)} %get-tuple-element.744, f32[256]{0:T(256)S(1)} %fusion.91, ...), kind=kLoop, calls=%fused_computation.35.clone.1 | loop fusion | flops 8910848 | bytes 6382592 | tf_op jit(solution)/shard_map/while/body/reduce_sum | solution.py:106
  150.3 1.2 subtract_log_fusion.8
  151.4 1.3 fusion.92
  152.7 2.2 fusion.94
  154.9 2.5 fusion.93
  157.4 1.3 fusion.95
  158.7 4.2 %fusion.96 = f32[16,128]{1,0:T(8,128)S(1)} fusion(f32[16,128,256]{2,1,0:T(8,128)S(1)} %get-tuple-element.748, f32[16,256,128]{1,0,2:T(8,128)S(1)} %fusion.95, f32[16,256]{1,0:T(8,128)S(1)} %add.491, f32[16,128]{1,0:T(8,128)S(1)} %get-tuple-element.743, f32[16,128]{1,0:T(8,128)S(1)} %get-tuple-element.744, f32[256]{0:T(256)S(1)} %fusion.91, ...), kind=kLoop, calls=%fused_computation.35.clone.1 | loop fusion | flops 8910848 | bytes 6382592 | tf_op jit(solution)/shard_map/while/body/reduce_sum | solution.py:106
  163.1 0.8 copy.69
  163.9 24.5 %scatter_custom_fusion = f32[65,8192]{0,1:T(8,128)} fusion(s32[4096]{0:T(1024)S(1)} %bitcast.103, f32[4096,65]{1,0:T(8,128)S(1)} %bitcast.99, f32[]{:T(128)} %constant.142.clone.1), kind=kCustom, calls=%fused_computation.73 | custom fusion | flops 266240 | bytes 2129924 | tf_op jit(solution)/shard_map/scatter-add | solution.py:160
  188.4 1.6 slice-done
  190.0 0.9 copy.65
  190.9 1.9 collective-permute-start.1
  192.9 13.7 %collective-permute-done.1 = f32[65,4096]{1,0:T(8,128)} collective-permute-done((f32[65,4096]{1,0:T(8,128)S(1)}, f32[65,4096]{1,0:T(8,128)}, u32[]{:S(2)}, u32[]{:S(2)}) %collective-permute-start.1) | collective-permute-done | bytes 1064992 | tf_op jit(solution)/shard_map/ppermute | solution.py:12
  206.6 1.8 copy.66
  208.4 3.1 %slice_add_fusion = f32[65,4096]{0,1:T(8,128)} fusion(f32[65,4096]{0,1:T(8,128)S(1)} %copy.66, f32[65,8192]{0,1:T(8,128)} %scatter_custom_fusion), kind=kLoop, calls=%fused_computation.72 | loop fusion | flops 266240 | bytes 3194880 | tf_op jit(solution)/shard_map/add | solution.py:163
  211.5 75.5 %reduce-scatter.2.cloned.1.call-done = f32[65,256]{0,1:T(8,128)} async-done(((f32[65,4096]{0,1:T(8,128)}), f32[65,256]{0,1:T(8,128)}) %reduce-scatter.2.cloned.1.call-update) | async-done | bytes 66576 | tf_op jit(solution)/shard_map/reduce_scatter | solution.py:162
  287.0 1.6 copy.67
  288.7 1.7 slice_reduce_fusion
  (72 shorter events, 3.5 us)
Async XLA Ops:
  7.2 122.7 %copy-start = (bf16[64,512]{1,0:T(8,128)(2,1)S(1)}, bf16[64,512]{1,0:T(8,128)(2,1)}, u32[]{:S(2)}) copy-start(bf16[64,512]{1,0:T(8,128)(2,1)} %param.18) | copy-start | bytes 196612
  7.2 87.2 %all-gather.3.cloned.1.call-start = ((), (), s32[]{:S(2)}) async-start(), calls=%async_computation.2 | async-start | bytes 2506752 | tf_op jit(solution)/shard_map/all_gather | solution.py:148
  8.1 12.4 %collective-permute-start = (f32[69,256]{1,0:T(8,128)S(1)}, f32[69,256]{1,0:T(8,128)S(1)}, u32[]{:S(2)}, u32[]{:S(2)}) collective-permute-start(f32[69,256]{1,0:T(8,128)S(1)} %get-tuple-element.528), channel_id=1, source_target_pairs={{0,1},{1,2},{2,3},{3,4},{4,5},{5,6},{6,7},{7,8},{8,9},{9,10},{10,1... | collective-permute-start | bytes 211976 | tf_op jit(solution)/shard_map/ppermute | solution.py:12
  21.2 265.9 %reduce-scatter.2.cloned.1.call-start = ((), (), s32[]{:S(2)}) async-start(), calls=%async_computation.1 | async-start | bytes 2228224 | tf_op jit(solution)/shard_map/reduce_scatter | solution.py:162
  116.9 1.2 copy-start.2
  129.9 2.2 copy-start.1
  188.4 1.6 slice-start
  190.9 15.6 %collective-permute-start.1 = (f32[65,4096]{1,0:T(8,128)S(1)}, f32[65,4096]{1,0:T(8,128)}, u32[]{:S(2)}, u32[]{:S(2)}) collective-permute-start(f32[65,4096]{1,0:T(8,128)S(1)} %copy.65), channel_id=1, source_target_pairs={{1,0},{2,1},{3,2},{4,3},{5,4},{6,5},{7,6},{8,7},{9,8},{10,9},{11,1... | collective-permute-start | bytes 3194888 | tf_op jit(solution)/shard_map/ppermute | solution.py:12
Sparse Core Ops, SparseCore 0:
  21.3 73.0 all-gather.2
  211.6 75.3 reduce-scatter.1
